TPU v7x, 32 devices: a whole 2x2x4 slice. The times are simulated.
32 devices in a mesh: blk: 8 (over z, y), grp: 4 (over x, core).
Axes of the slice: x: 2, y: 2, z: 4, core: 2. Of those that a mesh axis runs over, the one named last changes fastest.
Arguments:
- state: float32 [6, 131072], P(None, ('blk', 'grp')), may hold values from -6 to 6
- mass: float32 [131072], P(('blk', 'grp')), may hold values from 1.5258789e-06 to 3.8146973e-05
- active_index: int32 [8, 32], P('blk'), may hold values from 0 to 16383, as said below
- counts: int32 [8], P('blk'), may hold values from 8 to 32, as said below
Outputs:
- acc_jerk: float32 [6, 256], P(None, 'blk')
- potential: float32 [256], P('blk')
Inputs may be any that keep to these rules, and one draw needn't show every extreme that they name: `active_index`: each row holds 32 different star numbers of its slot block; only the first counts[b] entries of row b are active. `counts`: in every draw some slot is full, with 32 active stars.
All inputs are finite; a program needn't handle non-finite values.
Results may differ from a plain program's by a relative error of at most 0.0003.
Values sent between devices are 32-bit elements; how exact they have to be, the bound alone decides.
A program may use at most 64 MiB of HBM per device.

v0:
```python
import functools

import jax
import jax.numpy as jnp
from jax import lax
from jax.experimental import pallas as pl
from jax.experimental.pallas import tpu as pltpu
from jax.sharding import PartitionSpec as P

softening = 0.001
LANES = 128
MESH = pl.DeviceIdType.MESH
UNROLL = 8
SPREAD = 512


def pieces(rows):
    out = []
    for _ in range(3):
        piece = rows.astype(jnp.bfloat16).astype(jnp.float32)
        out.append(piece)
        rows = rows - piece
    return jnp.concatenate(out, axis=0)


def spread_chunk(state_ref, mass_ref, wide_ref, pick, chunk):
    parts = []
    for u in range(SPREAD // LANES):
        start = pl.multiple_of(chunk * SPREAD + u * LANES, LANES)
        rows = jnp.concatenate(
            [
                state_ref[:, pl.ds(start, LANES)],
                mass_ref[pl.ds(chunk * (SPREAD // LANES) + u, 1), :],
                jnp.zeros((1, LANES), jnp.float32),
            ],
            axis=0,
        )
        parts.append(pieces(rows).T)
    columns = jnp.concatenate(parts, axis=0).astype(jnp.bfloat16)
    wide = jnp.dot(columns, pick, preferred_element_type=jnp.float32)
    at = pl.ds(pl.multiple_of(chunk * SPREAD, SPREAD), SPREAD)
    for c in range(7):
        wide_ref[c, at, :] = wide[:, c * LANES : (c + 1) * LANES]


def turned(x, cap):
    return [x] + [pltpu.roll(x, k * cap, 1) for k in range(1, LANES // cap)]


def by_block(rows, cap):
    block = lax.broadcasted_iota(jnp.int32, rows[0].shape, 1) // cap
    out = rows[0]
    for b in range(1, len(rows)):
        out = jnp.where(block == b, rows[b], out)
    return out


def tile_terms(packed, wide_ref, begin, end, cap):
    size = LANES // cap
    high = 8 // size
    moved = turned(packed, cap)
    mine = []
    for c in range(6):
        rows = [moved[(b - c % size) % size][b * high + c // size :][:1] for b in range(size)]
        mine.append(jnp.broadcast_to(by_block(rows, cap), (8, LANES)))

    def body(step, totals):
        totals = list(totals)
        for u in range(UNROLL):
            at = pl.ds(pl.multiple_of((step * UNROLL + u) * 8, 8), 8)
            dx = [wide_ref[c, at, :] - mine[c] for c in range(3)]
            dv = [wide_ref[c, at, :] - mine[c] for c in range(3, 6)]
            raw = dx[0] * dx[0] + dx[1] * dx[1] + dx[2] * dx[2]
            weight = jnp.where(raw == 0.0, 0.0, wide_ref[6, at, :])
            inv = lax.rsqrt(raw + softening)
            square = inv * inv
            first = weight * inv
            third = first * square
            along = dx[0] * dv[0] + dx[1] * dv[1] + dx[2] * dv[2]
            ratio = (3.0 * along) * square
            for c in range(3):
                totals[c] = totals[c] + third * dx[c]
                totals[3 + c] = totals[3 + c] + third * (dv[c] - ratio * dx[c])
            totals[6] = totals[6] + first
        return tuple(totals)

    zero = jnp.zeros((8, LANES), jnp.float32)
    totals = lax.fori_loop(begin // (8 * UNROLL), end // (8 * UNROLL), body, (zero,) * 7)
    sums = [jnp.sum(t, axis=0, keepdims=True) for t in totals]
    moved = turned(jnp.concatenate(sums[:6] + [-sums[6], jnp.zeros((1, LANES), jnp.float32)], axis=0), cap)
    rows = []
    for b in range(size):
        for r in range(high):
            rows.append(by_block([moved[(q - b) % size][r * size + q :][:1] for q in range(size)], cap))
    return jnp.concatenate(rows, axis=0)


def each(first, last, do):
    if last - first <= 32:
        for i in range(first, last):
            do(i)
    else:
        pl.loop(first, last)(do)


def kernel(
    n_blk, n_grp, cap, state_in, mass_in, picks_in, counts_ref, out_ref, pot_ref,
    state_ref, mass_ref, picks_ref, load_sem, wide_ref, part_ref, own_in, list_ref, list_in, sum_ref, sum_in,
    own_s, own_r, list_s, list_r, sum_s, sum_r,
):
    blk, grp = lax.axis_index("blk"), lax.axis_index("grp")
    stars = state_ref.shape[1]
    size = LANES // cap
    high = 8 // size
    tiles = n_blk // size
    group = size * n_grp
    everyone = n_blk * n_grp
    tile, place = blk // size, blk % size
    me = blk * n_grp + grp

    def ahead(i):
        dt, dr, dg = i // group, (i % group) // n_grp, i % n_grp
        return ((tile + dt) % tiles) * size + (place + dr) % size, (grp + dg) % n_grp

    def behind(i):
        dt, dr, dg = i // group, (i % group) // n_grp, i % n_grp
        return ((tile + tiles - dt) % tiles) * size + (place + size - dr) % size, (grp + n_grp - dg) % n_grp

    barrier = pltpu.get_barrier_semaphore()

    for dt in range(1, tiles):
        pl.semaphore_signal(barrier, inc=1, device_id=ahead(dt * group), device_id_type=MESH)

    @pl.loop(1, group)
    def _(i):
        pl.semaphore_signal(barrier, inc=1, device_id=ahead(group - i), device_id_type=MESH)

    loads = [
        pltpu.make_async_copy(src, dst, load_sem.at[i])
        for i, (src, dst) in enumerate(
            [(state_in, state_ref), (mass_in, mass_ref), (picks_in, picks_ref)]
        )
    ]
    for copy in loads:
        copy.start()
    for copy in loads:
        copy.wait()

    picks = jnp.concatenate([picks_ref[...] - grp * stars] * size, axis=1)
    depth = 512
    row = lax.broadcasted_iota(jnp.int32, (depth, LANES), 0)
    found = jnp.zeros((18, LANES), jnp.float32)
    for k in range(stars // depth):
        hot = jnp.where(row + k * depth == picks, 1.0, 0.0).astype(jnp.bfloat16)
        rows = pieces(state_ref[:, k * depth : (k + 1) * depth]).astype(jnp.bfloat16)
        found = found + jnp.dot(rows, hot, preferred_element_type=jnp.float32)
    found = found[0:6] + found[6:12] + found[12:18]
    found = jnp.concatenate([found, jnp.zeros((2, LANES), jnp.float32)], axis=0)
    part = jnp.concatenate(
        [by_block([found[r * size + q :][:1] for q in range(size)], cap) for r in range(high)], axis=0
    )
    part_ref[...] = part

    source = lax.broadcasted_iota(jnp.int32, (24, 7 * LANES), 0) % 8
    target = lax.broadcasted_iota(jnp.int32, (24, 7 * LANES), 1) // LANES
    pick = jnp.where(source == target, 1.0, 0.0).astype(jnp.bfloat16)
    chunks = stars // SPREAD

    @pl.loop(0, chunks // 2)
    def _(chunk):
        spread_chunk(state_ref, mass_ref, wide_ref, pick, chunk)

    pl.semaphore_wait(barrier, group - 1 + tiles - 1)

    def share(i):
        return pltpu.make_async_remote_copy(
            src_ref=part_ref, dst_ref=own_in.at[i], send_sem=own_s.at[i], recv_sem=own_r.at[i],
            device_id=ahead(i), device_id_type=MESH,
        )

    def pass_on(dt):
        return pltpu.make_async_remote_copy(
            src_ref=list_ref, dst_ref=list_in.at[dt], send_sem=list_s.at[dt], recv_sem=list_r.at[dt],
            device_id=ahead(dt * group), device_id_type=MESH,
        )

    def give(i):
        return pltpu.make_async_remote_copy(
            src_ref=sum_ref.at[i // group, (i % group) // n_grp], dst_ref=sum_in.at[me], send_sem=sum_s.at[i],
            recv_sem=sum_r.at[me], device_id=behind(i), device_id_type=MESH,
        )

    def take(i):
        there = behind(i)
        at = there[0] * n_grp + there[1]
        return pltpu.make_async_remote_copy(
            src_ref=part_ref, dst_ref=sum_in.at[at], send_sem=sum_s.at[i], recv_sem=sum_r.at[at],
            device_id=there, device_id_type=MESH,
        )

    each(1, group, lambda i: share(i).start())

    @pl.loop(chunks // 2, chunks)
    def _(chunk):
        spread_chunk(state_ref, mass_ref, wide_ref, pick, chunk)

    each(1, group, lambda i: share(i).wait_recv())

    packed = []
    for dr in range(size):
        slot = part if dr == 0 else own_in[dr * n_grp]
        for dg in range(1, n_grp):
            slot = slot + own_in[dr * n_grp + dg]
        packed.append(slot)
    packed = jnp.concatenate(packed, axis=0)
    list_ref[...] = packed
    for dt in range(1, tiles):
        pass_on(dt).start()

    def hand_out(dt, terms):
        for dr in range(size):
            sum_ref[dt, dr] = terms[dr * high : (dr + 1) * high]

        each(dt * group + (dt == 0), (dt + 1) * group, lambda i: give(i).start())

    most = stars // 4 * 3
    terms = tile_terms(packed, wide_ref, 0, most, cap)
    for dt in range(1, tiles):
        pass_on(dt).wait_recv()
        hand_out(dt, tile_terms(list_in[dt], wide_ref, 0, stars, cap))
    terms = terms + tile_terms(packed, wide_ref, most, stars, cap)
    sum_in[me] = terms[:high]
    hand_out(0, terms)

    each(1, everyone, lambda i: take(i).wait_recv())

    total = sum_in[0]
    for k in range(1, everyone):
        total = total + sum_in[k]
    moved = turned(total, cap)
    rows = [moved[(size - c % size) % size][c // size :][:1, :cap] for c in range(7)]
    live = lax.broadcasted_iota(jnp.int32, (1, cap), 1) < counts_ref[0]
    out_ref[...] = jnp.where(live, jnp.concatenate(rows[:6], axis=0), 0.0)
    pot_ref[...] = jnp.where(live, rows[6], 0.0)

    each(1, everyone, lambda i: give(i).wait_send())

    each(1, group, lambda i: share(i).wait_send())

    for dt in range(1, tiles):
        pass_on(dt).wait_send()


def solution(mesh):
    n_blk, n_grp = mesh.shape["blk"], mesh.shape["grp"]

    def on_device(state, mass, active_index, counts):
        stars, cap = state.shape[1], active_index.shape[1]
        f32 = jnp.float32
        tile = (8 * cap // LANES, LANES)
        tiles = n_blk * cap // LANES
        near = n_grp * LANES // cap
        everyone = n_blk * n_grp
        sems = pltpu.SemaphoreType.DMA
        vmem = pl.BlockSpec(memory_space=pltpu.VMEM)
        out, pot = pl.pallas_call(
            functools.partial(kernel, n_blk, n_grp, cap),
            out_shape=(jax.ShapeDtypeStruct((6, cap), f32), jax.ShapeDtypeStruct((1, cap), f32)),
            in_specs=[pl.BlockSpec(memory_space=pltpu.HBM)] * 3 + [pl.BlockSpec(memory_space=pltpu.SMEM)],
            out_specs=(vmem, vmem),
            scratch_shapes=[
                pltpu.VMEM((6, stars), f32),
                pltpu.VMEM((stars // LANES, LANES), f32),
                pltpu.VMEM((1, cap), jnp.int32),
                sems((3,)),
                pltpu.VMEM((7, stars, LANES), f32),
                pltpu.VMEM(tile, f32),
                pltpu.VMEM((near, *tile), f32),
                pltpu.VMEM((8, LANES), f32),
                pltpu.VMEM((tiles, 8, LANES), f32),
                pltpu.VMEM((tiles, LANES // cap, *tile), f32),
                pltpu.VMEM((everyone, *tile), f32),
                sems((near,)), sems((near,)), sems((tiles,)), sems((tiles,)), sems((everyone,)), sems((everyone,)),
            ],
            compiler_params=pltpu.CompilerParams(
                collective_id=0, has_side_effects=True, vmem_limit_bytes=40 * 1024 * 1024
            ),
        )(*(
            pltpu.with_memory_space_constraint(x, pltpu.HBM)
            for x in (state, mass.reshape(stars // LANES, LANES), active_index)
        ), counts)
        return out, pot.reshape(cap)

    placed = (P(None, ("blk", "grp")), P(("blk", "grp")), P("blk", None), P("blk"))
    return jax.shard_map(
        on_device, mesh=mesh, in_specs=placed, out_specs=(P(None, "blk"), P("blk")), check_vma=False
    )
```

profile of v0, /device:TPU:0, one launch (start us, length us, event | category | flops | bytes accessed | tf_op | source)
XLA Modules:
  0.0 24.6 jit_solution(16289062796856784243)
XLA Ops:
  1.3 22.2 %shard_map.59 = (f32[6,32]{1,0:T(8,128)S(1)}, f32[1,32]{1,0:T(1,128)S(1)}) custom-call(f32[6,4096]{1,0:T(8,128)} %state_in.1, f32[32,128]{1,0:T(8,128)} %bitcast.3, s32[1,32]{1,0:T(1,128)} %picks_in.1, s32[1]{0:T(128)S(6)} %copy.8.counts_ref), custom_call_target="tpu_custom_call" | custom-call | tf_op jit(solution)/shard_map/pallas_call | solution.py:266
  23.5 0.6 %copy.9 = f32[6,32]{1,0:T(8,128)} copy(f32[6,32]{1,0:T(8,128)S(1)} %get-tuple-element.8) | data formatting | bytes 1536
  24.1 0.5 %copy.10 = f32[32]{0:T(128)} copy(f32[32]{0:T(128)S(1)} %bitcast.2) | data formatting | bytes 256
where the time goes:
time: 24.7 us; the launch traced here: 24.6 us
  Pallas kernels  22.2 us (90%)
  between operations  1.29 us (5%)
  local copies, waits for them, and re-layouts  1.11 us (4%)
    pallas_call x1, Pallas kernels, on_device(): pl.pallas_call(functools.partial(kernel, n_blk, n_grp, cap), out_shape=(j...  22.2 us
    unnamed x2, local copies, waits for them, and re-layouts  1.11 us

commit v1 on v0

v1 whole, which is shorter than its diff:
```python
import functools

import jax
import jax.numpy as jnp
from jax import lax
from jax.experimental import pallas as pl
from jax.experimental.pallas import tpu as pltpu
from jax.sharding import PartitionSpec as P

softening = 0.001
LANES = 128
ROWS = 8
CHUNKS = 32
MESH = pl.DeviceIdType.MESH


def pieces(rows):
    out = []
    for _ in range(3):
        piece = rows.astype(jnp.bfloat16).astype(jnp.float32)
        out.append(piece)
        rows = rows - piece
    return jnp.concatenate(out, axis=0)


def turned(x, cap):
    return [x] + [pltpu.roll(x, k * cap, 1) for k in range(1, LANES // cap)]


def by_block(rows, cap):
    block = lax.broadcasted_iota(jnp.int32, rows[0].shape, 1) // cap
    out = rows[0]
    for b in range(1, len(rows)):
        out = jnp.where(block == b, rows[b], out)
    return out


def bits(x, size):
    out = []
    at = 1
    while at < size:
        out.append(lax.rem(lax.div(x, jnp.int32(at)), jnp.int32(2)))
        at *= 2
    return out


def flipped(own, k):
    total = jnp.int32(0)
    for b, bit in enumerate(own):
        if isinstance(k, int):
            total = total + (1 << b) * ((1 - bit) if (k >> b) & 1 else bit)
        else:
            total = total + (1 << b) * lax.rem(bit + lax.div(k, jnp.int32(1 << b)), jnp.int32(2))
    return total


def each(first, last, do):
    if last - first <= 32:
        for i in range(first, last):
            do(i)
    else:
        pl.loop(first, last)(do)


def split(i, size):
    if isinstance(i, int):
        return i // size, i % size
    return lax.div(i, jnp.int32(size)), lax.rem(i, jnp.int32(size))


def group_terms(state_ref, mass_ref, mine, stars):
    def step(base, totals):
        totals = list(totals)
        for k in range(CHUNKS):
            at = pl.ds(pl.multiple_of(base * (CHUNKS * LANES) + k * LANES, LANES), LANES)
            star = [jnp.broadcast_to(state_ref[c : c + 1, at], (ROWS, LANES)) for c in range(6)]
            mass = jnp.broadcast_to(mass_ref[pl.ds(base * CHUNKS + k, 1), :], (ROWS, LANES))
            dx = [star[c] - mine[c] for c in range(3)]
            dv = [star[c] - mine[c] for c in range(3, 6)]
            raw = dx[0] * dx[0] + dx[1] * dx[1] + dx[2] * dx[2]
            weight = jnp.where(raw == 0.0, 0.0, mass)
            inv = lax.rsqrt(raw + softening)
            square = inv * inv
            first = weight * inv
            third = first * square
            along = dx[0] * dv[0] + dx[1] * dv[1] + dx[2] * dv[2]
            ratio = along * square
            for c in range(3):
                pull = third * dx[c]
                totals[c] = totals[c] + pull
                totals[3 + c] = totals[3 + c] + third * dv[c]
                totals[7 + c] = totals[7 + c] + ratio * pull
            totals[6] = totals[6] + first
        return tuple(totals)

    zero = (jnp.zeros((ROWS, LANES), jnp.float32),) * 10
    steps = stars // (CHUNKS * LANES)
    totals = step(0, zero) if steps == 1 else lax.fori_loop(0, steps, step, zero)
    jerk = [totals[3 + c] - 3.0 * totals[7 + c] for c in range(3)]
    return [*totals[:3], *jerk, -totals[6]]


def widen(tall_ref, mine_ref, m, pairs, cap):
    slot, pair = split(m, pairs)
    for h in range(2):
        for c in range(6):
            start = (c % (LANES // cap)) * cap + (2 * pair + h) * ROWS
            block = tall_ref[slot, pl.ds(pl.multiple_of(start, ROWS), ROWS), :]
            column = block[:, c // (LANES // cap) : c // (LANES // cap) + 1]
            mine_ref[m, h, c] = jnp.broadcast_to(column, (ROWS, LANES))


def narrow(acc_ref, line_ref, m):
    line_ref[m] = jnp.sum(acc_ref[m].T, axis=0, keepdims=True)


def kernel(
    n_blk, n_grp, cap, near, state_in, mass_in, picks_in, counts_in, out_ref,
    state_ref, mass_ref, picks_ref, counts_ref, load_sem, part_ref, own_in, list_ref, list_in,
    tall_ref, mine_ref, acc_ref, line_ref, sum_ref, sum_in, own_s, own_r, list_s, list_r, sum_s, sum_r,
):
    blk, grp = lax.axis_index("blk"), lax.axis_index("grp")
    stars = state_ref.shape[1]
    size = LANES // cap
    high = 8 // size
    pairs = cap // (2 * ROWS)
    group = near * n_grp
    tiles = n_blk // near
    everyone = n_blk * n_grp
    blk_bits, grp_bits = bits(blk, n_blk), bits(grp, n_grp)

    def partner(i):
        db, dg = split(i, n_grp)
        return flipped(blk_bits, db), flipped(grp_bits, dg)

    loads = [
        pltpu.make_async_copy(src, dst, load_sem.at[i])
        for i, (src, dst) in enumerate(
            [(picks_in, picks_ref), (state_in, state_ref), (mass_in, mass_ref), (counts_in, counts_ref)]
        )
    ]
    for copy in loads:
        copy.start()

    barrier = pltpu.get_barrier_semaphore()

    def greet(i):
        pl.semaphore_signal(barrier, inc=1, device_id=partner(i), device_id_type=MESH)

    each(1, group, lambda i: greet(group - i))
    for dt in range(1, tiles):
        greet(dt * group)

    def clear(m):
        for h in range(2):
            acc_ref[m, h * 64 : h * 64 + ROWS, :] = jnp.zeros((ROWS, LANES), jnp.float32)

    each(0, pairs * n_blk + 1, clear)

    with jax.named_scope("loadwait"):
        for copy in loads:
            copy.wait()

    picks = jnp.concatenate([picks_ref[...] - grp * stars] * size, axis=1)
    depth = 512
    row = lax.broadcasted_iota(jnp.int32, (depth, LANES), 0)
    found = jnp.zeros((18, LANES), jnp.float32)
    for k in range(stars // depth):
        hot = jnp.where(row + k * depth == picks, 1.0, 0.0).astype(jnp.bfloat16)
        rows = pieces(state_ref[:, k * depth : (k + 1) * depth]).astype(jnp.bfloat16)
        found = found + jnp.dot(rows, hot, preferred_element_type=jnp.float32)
    found = found[0:6] + found[6:12] + found[12:18]
    found = jnp.concatenate([found, jnp.zeros((2, LANES), jnp.float32)], axis=0)
    part = jnp.concatenate(
        [by_block([found[r * size + q :][:1] for q in range(size)], cap) for r in range(high)], axis=0
    )
    part_ref[...] = part
    own_in[0] = part

    with jax.named_scope("barwait"):
        pl.semaphore_wait(barrier, group - 1 + tiles - 1)

    def share(i):
        return pltpu.make_async_remote_copy(
            src_ref=part_ref, dst_ref=own_in.at[i], send_sem=own_s, recv_sem=own_r,
            device_id=partner(i), device_id_type=MESH,
        )

    def pass_on(dt):
        return pltpu.make_async_remote_copy(
            src_ref=list_ref, dst_ref=list_in.at[dt], send_sem=list_s.at[dt], recv_sem=list_r.at[dt],
            device_id=partner(dt * group), device_id_type=MESH,
        )

    def give(i):
        return pltpu.make_async_remote_copy(
            src_ref=sum_ref.at[split(i, n_grp)[0]], dst_ref=sum_in.at[i], send_sem=sum_s, recv_sem=sum_r,
            device_id=partner(i), device_id_type=MESH,
        )

    def whole(ref, count, send_sem, recv_sem):
        span = ref.at[pl.ds(1, count - 1)]
        return pltpu.make_async_remote_copy(
            src_ref=span, dst_ref=span, send_sem=send_sem, recv_sem=recv_sem,
            device_id=partner(1), device_id_type=MESH,
        )

    each(1, group, lambda i: share(group - i).start())

    def turn(slot, listed):
        tall_ref[slot] = jnp.concatenate([listed, jnp.zeros((8 - high, LANES), jnp.float32)], axis=0).T

    def sweep(first, last):
        widen(tall_ref, mine_ref, first * pairs, pairs, cap)

        @pl.loop(first * pairs, last * pairs)
        def _(m):
            mine = [[mine_ref[m, h, c] for c in range(6)] for h in range(2)]
            narrow(acc_ref, line_ref, m)
            widen(tall_ref, mine_ref, jnp.minimum(m + 1, last * pairs - 1), pairs, cap)
            for h in range(2):
                for c, total in enumerate(group_terms(state_ref, mass_ref, mine[h], stars)):
                    acc_ref[m + 1, pl.ds(h * 64 + (7 - c) * ROWS, ROWS), :] = total

        narrow(acc_ref, line_ref, last * pairs)

        def gather(slot):
            for p in range(pairs):
                sum_ref[slot, p : p + 1] = line_ref[slot * pairs + p + 1]

        each(first, last, gather)
        each(first * n_grp + (first == 0), last * n_grp, lambda i: give(i).start())

    with jax.named_scope("sharewait"):
        whole(own_in, group, own_s, own_r).wait_recv()
    with jax.named_scope("lists"):
        lists = []
        for slot in range(near):
            listed = own_in[slot * n_grp]
            for dg in range(1, n_grp):
                listed = listed + own_in[slot * n_grp + dg]
            lists.append(listed)
            list_ref[slot] = listed
        for dt in range(1, tiles):
            pass_on(dt).start()
        for slot in range(near):
            turn(slot, lists[slot])
    with jax.named_scope("near"):
        sweep(1, near)
    for dt in range(1, tiles):
        with jax.named_scope("passwait"):
            pass_on(dt).wait_recv()
        with jax.named_scope("far"):
            for slot in range(near):
                turn(dt * near + slot, list_in[dt, slot])
            cut = dt * near + near // 2
            sweep(cut, (dt + 1) * near)
            sweep(dt * near, cut)
    with jax.named_scope("own"):
        sweep(0, 1)

    sum_in[0] = sum_ref[0]
    with jax.named_scope("takewait"):
        whole(sum_in, everyone, sum_s, sum_r).wait_recv()

    with jax.named_scope("final"):
        sums = [sum_in[k] for k in range(4)]
        for k in range(4, everyone):
            sums[k % 4] = sums[k % 4] + sum_in[k]
        total = (sums[0] + sums[1]) + (sums[2] + sums[3])
        block = lax.broadcasted_iota(jnp.int32, (ROWS, LANES), 1) // ROWS
        table = jnp.zeros((ROWS, LANES), jnp.float32)
        for p in range(pairs):
            line = jnp.broadcast_to(total[p : p + 1], (ROWS, LANES))
            for h in range(2):
                g = 2 * p + h
                moved = pltpu.roll(line, (g * ROWS - h * 64 - 56) % LANES, 1)
                moved = pltpu.roll(moved, 0, 1, stride=ROWS, stride_axis=0)
                table = jnp.where(block == g, moved, table)
        live = lax.broadcasted_iota(jnp.int32, (ROWS, LANES), 1) < counts_ref[...]
        out_ref[...] = jnp.where(live, table, 0.0)

    whole(own_in, group, own_s, own_r).wait_send()
    for dt in range(1, tiles):
        pass_on(dt).wait_send()
    whole(sum_in, everyone, sum_s, sum_r).wait_send()


def part_out(cap, table_ref, out_ref, pot_ref):
    out_ref[...] = table_ref[:6, :cap]
    pot_ref[...] = table_ref[6:7, :cap]


def solution(mesh):
    n_blk, n_grp = mesh.shape["blk"], mesh.shape["grp"]

    def on_device(state, mass, active_index, counts):
        stars, cap = state.shape[1], active_index.shape[1]
        f32 = jnp.float32
        tile = (8 * cap // LANES, LANES)
        everyone = n_blk * n_grp
        pairs = cap // (2 * ROWS)
        near = min(n_blk, LANES // cap)
        tiles = n_blk // near
        sems = pltpu.SemaphoreType.DMA
        vmem = pl.BlockSpec(memory_space=pltpu.VMEM)
        table = pl.pallas_call(
            functools.partial(kernel, n_blk, n_grp, cap, near),
            out_shape=jax.ShapeDtypeStruct((ROWS, LANES), f32),
            in_specs=[pl.BlockSpec(memory_space=pltpu.HBM)] * 3 + [pl.BlockSpec(memory_space=pl.ANY)],
            out_specs=vmem,
            scratch_shapes=[
                pltpu.VMEM((6, stars), f32),
                pltpu.VMEM((stars // LANES, LANES), f32),
                pltpu.VMEM((1, cap), jnp.int32),
                pltpu.VMEM((1, 1), jnp.int32),
                sems((4,)),
                pltpu.VMEM(tile, f32),
                pltpu.VMEM((near * n_grp, *tile), f32),
                pltpu.VMEM((near, *tile), f32),
                pltpu.VMEM((tiles, near, *tile), f32),
                pltpu.VMEM((n_blk, LANES, 8), f32),
                pltpu.VMEM((n_blk * pairs, 2, 6, ROWS, LANES), f32),
                pltpu.VMEM((n_blk * pairs + 1, LANES, LANES), f32),
                pltpu.VMEM((n_blk * pairs + 1, 1, LANES), f32),
                pltpu.VMEM((n_blk, *tile), f32),
                pltpu.VMEM((everyone, *tile), f32),
                sems(()), sems(()), sems((tiles,)), sems((tiles,)), sems(()), sems(()),
            ],
            compiler_params=pltpu.CompilerParams(
                collective_id=0, has_side_effects=True, vmem_limit_bytes=40 * 1024 * 1024
            ),
        )(*(
            pltpu.with_memory_space_constraint(x, pltpu.HBM)
            for x in (state, mass.reshape(stars // LANES, LANES), active_index)
        ), counts.reshape(1, 1))
        out, pot = pl.pallas_call(
            functools.partial(part_out, cap),
            out_shape=(jax.ShapeDtypeStruct((6, cap), f32), jax.ShapeDtypeStruct((1, cap), f32)),
            in_specs=[vmem],
            out_specs=(vmem, vmem),
            compiler_params=pltpu.CompilerParams(vmem_limit_bytes=1024 * 1024),
        )(table)
        return out, pot.reshape(cap)

    placed = (P(None, ("blk", "grp")), P(("blk", "grp")), P("blk", None), P("blk"))
    return jax.shard_map(
        on_device, mesh=mesh, in_specs=placed, out_specs=(P(None, "blk"), P("blk")), check_vma=False
    )
```

time: 24.7 us -> 22.4 us (0.907)
  Pallas kernels: 22.2 us -> 21 us
  local copies, waits for them, and re-layouts: 1.11 us -> 0 us
    pallas_call x1 -> x2, Pallas kernels: 22.2 us -> 21 us  [the longest x1 20.4 us: on_device(): pl.pallas_call(functools.partial(kernel, n_blk, n_grp, cap, near), out_sh...]
    unnamed x2 -> x0, local copies, waits for them, and re-layouts: 1.11 us -> none
where the time goes in v1:
time: 22.4 us; the launch traced here: 22.3 us
  Pallas kernels  21 us (94%)
  between operations  1.28 us (6%)
    pallas_call x1, Pallas kernels, on_device(): pl.pallas_call(functools.partial(kernel, n_blk, n_grp, cap, near), out_sh...  20.4 us
    pallas_call x1, Pallas kernels, on_device(): pl.pallas_call(functools.partial(part_out, cap), out_shape=(jax.ShapeDtyp...  0.6 us

profile of v1, /device:TPU:0, one launch (start us, length us, event | category | flops | bytes accessed | tf_op | source)
XLA Modules:
  0.0 22.3 jit_solution(17449866584169131321)
XLA Ops:
  1.3 20.4 %shard_map.59.table_ref = f32[8,128]{1,0:T(8,128)S(1)} custom-call(f32[6,4096]{1,0:T(8,128)} %state_in.1, f32[32,128]{1,0:T(8,128)} %bitcast.4, s32[1,32]{1,0:T(1,128)} %picks_in.1, s32[1,1]{1,0:T(1,128)} %bitcast.3.counts_in), custom_call_target="tpu_custom_call" | custom-call | tf_op jit(solution)/shard_map/pallas_call | solution.py:307
  21.7 0.6 %shard_map.60 = (f32[6,32]{1,0:T(8,128)}, f32[1,32]{1,0:T(1,128)}) custom-call(f32[8,128]{1,0:T(8,128)S(1)} %shard_map.59.table_ref), custom_call_target="tpu_custom_call" | custom-call | tf_op jit(solution)/shard_map/pallas_call | solution.py:337
